TPU v7x, 32 devices: a whole 2x2x4 slice. The times are simulated.
32 devices in a mesh: tm: 16 (over z, y, core), band: 2 (over x).
Axes of the slice: x: 2, y: 2, z: 4, core: 2. Of those that a mesh axis runs over, the one named last changes fastest.
Arguments:
- phonon: float32 [32, 256, 256], P('tm', 'band'), may hold values from -4 to 4
- momentum: float32 [32, 256, 256], P('tm', 'band'), may hold values from -6 to 6
- source: float32 [32, 256, 256], P('tm', 'band'), may hold values from -6 to 6
- guess: float32 [32, 256, 256], P('tm', 'band'), may hold values from -4 to 4
- bonds: int32 [2, 256, 256], P(None, 'band'), may hold values 0 or 1
Outputs:
- solution: float32 [32, 256, 256], P('tm', 'band')
- momentum_new: float32 [32, 256, 256], P('tm', 'band')
All inputs are finite; a program needn't handle non-finite values. No bound on the sum of `bonds` on one device may be relied on, other than what follows from the above.
Results may differ from a plain program's by a relative error of at most 0.000064.
Values sent between devices are 32-bit elements; how exact they have to be, the bound alone decides.
No kernel may reach another device: no remote copies, remote signals or barrier semaphores. Data moves between devices by JAX's collectives and lax.ppermute only.
A program may use at most 64 MiB of HBM per device.

v0:
```python
import math
import jax
import jax.numpy as jnp
from jax import lax
from jax.sharding import PartitionSpec as P

ORDER = 24
hop_angle = 0.3
coupling = 0.2
stiffness = 1.0
mass_term = 0.5
relaxation = 0.25
step_size = 0.25
cheb_base = 4.03
cheb_slope = 0.5
half_width = 4.0
deep_width = 4


def extended(value, sides, width):
    for axis, dim in sides:
        size, length = (lax.axis_size(axis), value.shape[dim])
        up = [(i, (i + 1) % size) for i in range(size)]
        down = [(j, i) for i, j in up]
        last = lax.slice_in_dim(value, length - width, length, axis=dim)
        leading = lax.slice_in_dim(value, 0, width, axis=dim)
        before = lax.ppermute(last, axis, up)
        after = lax.ppermute(leading, axis, down)
        value = jnp.concatenate([before, value, after], axis=dim)
    return value


def passed_along(value, axis, by):
    size = lax.axis_size(axis)
    return lax.ppermute(value, axis, [(i, (i + by) % size) for i in range(size)])


def dft_basis(length_total):
    rows = lax.broadcasted_iota(jnp.int32, (length_total, length_total), 0)
    columns = lax.broadcasted_iota(jnp.int32, (length_total, length_total), 1)
    phase = (2 * (rows // 2) + 1) * columns % (2 * length_total)
    angle = phase.astype(jnp.float32) * (math.pi / length_total)
    return math.sqrt(2.0 / length_total) * jnp.where(rows % 2 == 0, jnp.cos(angle), jnp.sin(angle))


def cheb_centre(index, length_total):
    angle = (2 * (index // 2) + 1).astype(jnp.float32) * (math.pi / length_total)
    return cheb_base + cheb_slope * (1.0 - jnp.cos(angle))


def pair_tables(horizontal, vertical, vertical_prev, row_even, column_even):
    horizontal_prev = jnp.roll(horizontal, 1, 1)
    vertical_up = jnp.roll(vertical, 1, 0)
    strengths = (
        jnp.where(column_even, horizontal, horizontal_prev),
        jnp.where(column_even, horizontal_prev, horizontal),
        jnp.where(row_even, vertical, vertical_up),
        jnp.where(row_even, vertical_prev, vertical),
    )
    return tuple(
        ((jnp.cosh(hop_angle * strength), jnp.sinh(hop_angle * strength)) for strength in strengths)
    )


def partner_of(vector, colour, row_even, column_even):
    if colour == 0:
        return jnp.where(column_even, jnp.roll(vector, -1, 2), jnp.roll(vector, 1, 2))
    if colour == 1:
        return jnp.where(column_even, jnp.roll(vector, 1, 2), jnp.roll(vector, -1, 2))
    if colour == 2:
        return jnp.where(row_even, jnp.roll(vector, -1, 1), jnp.roll(vector, 1, 1))
    padded = extended(vector, (("band", 1),), 1)
    return jnp.where(row_even, padded[:, :-2], padded[:, 2:])


def to_spectrum(piece):
    basis = dft_basis(piece.shape[0])
    return jnp.einsum("kl,lrc->krc", basis, piece, precision=lax.Precision.HIGHEST)


def to_slices(piece):
    basis = dft_basis(piece.shape[0])
    return jnp.einsum("kl,krc->lrc", basis, piece, precision=lax.Precision.HIGHEST)


def shards(phonon, momentum, source, guess, bonds):
    slice_count, row_count, col_count = guess.shape
    cycle_size = lax.axis_size("tm")
    position = lax.axis_index("tm")
    grid_shape = (row_count, col_count)
    row_even = lax.broadcasted_iota(jnp.int32, grid_shape, 0) % 2 == 0
    column_even = lax.broadcasted_iota(jnp.int32, grid_shape, 1) % 2 == 0
    edge_bonds = passed_along(bonds[1][-1:], "band", 1)
    vertical_prev = jnp.concatenate([edge_bonds, bonds[1][:-1]], 0)
    tables = pair_tables(
        bonds[0].astype(jnp.float32),
        bonds[1].astype(jnp.float32),
        vertical_prev.astype(jnp.float32),
        row_even,
        column_even,
    )

    def apply_pairs(vector, colours):
        for colour in colours:
            cosh_part, sinh_part = tables[colour]
            vector = cosh_part * vector + sinh_part * partner_of(
                vector, colour, row_even, column_even
            )
        return vector

    phonon_rims = extended(phonon, (("tm", 0),), 1)
    factor_wide = jnp.exp(-coupling * phonon_rims)
    expo = factor_wide[1:-1]
    first_sign = jnp.where(position == 0, -1.0, 1.0).astype(jnp.float32)
    last_sign = jnp.where(position == cycle_size - 1, -1.0, 1.0).astype(jnp.float32)

    def from_prev(piece):
        return passed_along(piece, "tm", 1) * first_sign

    def from_after(piece):
        return passed_along(piece, "tm", -1) * last_sign

    applied = apply_pairs(expo * guess, (0, 1, 2, 3))
    link = guess - jnp.concatenate([from_prev(applied[-1:]), applied[:-1]], 0)
    shifted = jnp.concatenate([link[1:], from_after(link[:1])], 0)
    normal = link - expo * apply_pairs(shifted, (3, 2, 1, 0))
    residual = source - normal
    mixed = to_spectrum(lax.all_to_all(residual, "tm", split_axis=1, concat_axis=0, tiled=True))
    spectrum = lax.all_to_all(mixed, "tm", split_axis=0, concat_axis=1, tiled=True)
    freq_index = position * slice_count + jnp.arange(slice_count, dtype=jnp.int32)
    centre = cheb_centre(freq_index, slice_count * cycle_size)[:, None, None]
    ratio = centre / half_width
    start = (jnp.zeros_like(spectrum), spectrum, spectrum / centre, 1.0 / ratio)

    def sweep_block(counter, carry):
        accum, remaining, direction, weight_now = carry
        stacked = extended(jnp.stack([remaining, direction]), (("band", 2),), deep_width)
        rem_wide = stacked[0]
        dir_wide = stacked[1]
        for inner in range(deep_width):
            offset = deep_width - inner
            middle = dir_wide[:, 1:-1]
            beside_all = (
                dir_wide[:, :-2]
                + dir_wide[:, 2:]
                + jnp.roll(middle, 1, 2)
                + jnp.roll(middle, -1, 2)
            )
            accum = accum + dir_wide[:, offset : offset + row_count]
            rem_wide = rem_wide[:, 1:-1] - (centre * middle - beside_all)
            weight_new = 1.0 / (2.0 * ratio - weight_now)
            dir_wide = weight_new * weight_now * middle + 2.0 * weight_new / half_width * rem_wide
            weight_now = weight_new
        return (accum, rem_wide, dir_wide, weight_now)

    accum = lax.fori_loop(0, ORDER // deep_width, sweep_block, start)[0]
    mixed_back = to_slices(lax.all_to_all(accum, "tm", split_axis=1, concat_axis=0, tiled=True))
    timed = lax.all_to_all(mixed_back, "tm", split_axis=0, concat_axis=1, tiled=True)
    solution = guess + relaxation * timed
    propagated = apply_pairs(expo * solution, (0, 1, 2, 3))
    image = solution - jnp.concatenate([from_prev(propagated[-1:]), propagated[:-1]], 0)
    pulled = apply_pairs(jnp.concatenate([image[1:], from_after(image[:1])], 0), (3, 2, 1, 0))
    fermion_force = -2.0 * coupling * expo * solution * pulled
    boson_force = (
        stiffness * (2.0 * phonon - phonon_rims[:-2] - phonon_rims[2:]) + mass_term * phonon
    )
    momentum_new = momentum - step_size * (boson_force + fermion_force)
    return (solution, momentum_new)


def solution(mesh):
    return jax.shard_map(
        shards,
        mesh=mesh,
        in_specs=(
            P("tm", "band", None),
            P("tm", "band", None),
            P("tm", "band", None),
            P("tm", "band", None),
            P(None, "band", None),
        ),
        out_specs=(P("tm", "band", None), P("tm", "band", None)),
        check_vma=False,
    )
```

profile of v0, /device:TPU:0, one launch (start us, length us, event | category | flops | bytes accessed | tf_op | source)
XLA Modules:
  0.0 157.5 jit_solution(9558485487474373816)
XLA Ops:
  1.3 3.0 %collective-permute-start.2 = (s32[1,256]{1,0:T(1,128)S(1)}, s32[1,256]{1,0:T(1,128)S(1)}, u32[]{:S(2)}, u32[]{:S(2)}) collective-permute-start(s32[1,256]{1,0:T(1,128)S(1)} %slice_bitcast_fusion.4), channel_id=1, source_target_pairs={{0,1},{1,0},{2,3},{3,2},{4,5},{5,4},{6,7},{7,6},{8,9},{9,8},{10,11... | collective-permute-start | bytes 3080 | tf_op jit(solution)/shard_map/ppermute | solution.py:35
  5.4 4.4 %collective-permute-start.4 = (f32[1,128,256]{2,1,0:T(8,128)S(1)}, f32[1,128,256]{2,1,0:T(8,128)S(1)}, u32[]{:S(2)}, u32[]{:S(2)}) collective-permute-start(f32[1,128,256]{2,1,0:T(8,128)S(1)} %get-tuple-element.314), channel_id=1, source_target_pairs={{2,0},{4,2},{6,4},{8,6},{10,8},{12,10},{14,12},{16,14},{18,16},{20... | collective-permute-start | bytes 393224 | tf_op jit(solution)/shard_map/ppermute | solution.py:28
  10.9 1.7 %collective-permute-done.3 = f32[1,128,256]{2,1,0:T(8,128)S(1)} collective-permute-done((f32[1,128,256]{2,1,0:T(8,128)S(1)}, f32[1,128,256]{2,1,0:T(8,128)S(1)}, u32[]{:S(2)}, u32[]{:S(2)}) %collective-permute-start.3) | collective-permute-done | bytes 131104 | tf_op jit(solution)/shard_map/ppermute | solution.py:27
  13.7 2.0 %collective-permute-start.6 = (f32[2,1,256]{2,1,0:T(1,128)S(1)}, f32[2,1,256]{2,1,0:T(1,128)S(1)}, u32[]{:S(2)}, u32[]{:S(2)}) collective-permute-start(f32[2,1,256]{2,1,0:T(1,128)S(1)} %get-tuple-element.298), channel_id=1, source_target_pairs={{1,0},{0,1},{3,2},{2,3},{5,4},{4,5},{7,6},{6,7},{9,8},{8,9},{11,10... | collective-permute-start | bytes 6152 | tf_op jit(solution)/shard_map/ppermute | solution.py:28
  15.7 1.6 collective-permute-done.5
  17.5 7.1 %collective-permute-done.7 = f32[1,128,256]{2,1,0:T(8,128)S(1)} collective-permute-done((f32[1,128,256]{2,1,0:T(8,128)S(1)}, f32[1,128,256]{2,1,0:T(8,128)S(1)}, u32[]{:S(2)}, u32[]{:S(2)}) %collective-permute-start.7) | collective-permute-done | bytes 131104 | tf_op jit(solution)/shard_map/ppermute | solution.py:35
  24.8 2.5 %collective-permute-done.8 = f32[1,128,256]{2,1,0:T(8,128)S(1)} collective-permute-done((f32[1,128,256]{2,1,0:T(8,128)S(1)}, f32[1,128,256]{2,1,0:T(8,128)S(1)}, u32[]{:S(2)}, u32[]{:S(2)}) %collective-permute-start.8) | collective-permute-done | bytes 131104 | tf_op jit(solution)/shard_map/ppermute | solution.py:35
  27.3 2.0 %collective-permute-start.9 = (f32[2,1,256]{2,1,0:T(1,128)S(1)}, f32[2,1,256]{2,1,0:T(1,128)S(1)}, u32[]{:S(2)}, u32[]{:S(2)}) collective-permute-start(f32[2,1,256]{2,1,0:T(1,128)S(1)} %get-tuple-element.291), channel_id=1, source_target_pairs={{0,1},{1,0},{2,3},{3,2},{4,5},{5,4},{6,7},{7,6},{8,9},{9,8},{10,11... | collective-permute-start | bytes 6152 | tf_op jit(solution)/shard_map/ppermute | solution.py:27
  31.0 2.0 %collective-permute-done.10 = f32[2,1,256]{2,1,0:T(1,128)S(1)} collective-permute-done((f32[2,1,256]{2,1,0:T(1,128)S(1)}, f32[2,1,256]{2,1,0:T(1,128)S(1)}, u32[]{:S(2)}, u32[]{:S(2)}) %collective-permute-start.10) | collective-permute-done | bytes 2080 | tf_op jit(solution)/shard_map/ppermute | solution.py:28
  35.9 4.5 %all-to-all-start = ((f32[2,128,256]{2,0,1:T(2,128)}), f32[2,128,256]{2,0,1:T(2,128)S(1)}, u32[]{:S(2)}, u32[]{:S(2)}) async-start(f32[2,128,256]{2,0,1:T(2,128)} %copy.43), calls=%async_computation | async-start | bytes 524288 | tf_op jit(solution)/shard_map/all_to_all | solution.py:128
  40.4 10.0 %all-to-all-done = f32[2,128,256]{2,0,1:T(2,128)S(1)} async-done(((f32[2,128,256]{2,0,1:T(2,128)}), f32[2,128,256]{2,0,1:T(2,128)S(1)}, u32[]{:S(2)}, u32[]{:S(2)}) %all-to-all-start) | async-done | bytes 262176 | tf_op jit(solution)/shard_map/all_to_all | solution.py:128
  52.0 3.5 %all-to-all-start.1 = ((f32[32,8,256]{2,1,0:T(8,128)}), f32[32,8,256]{2,1,0:T(8,128)S(1)}, u32[]{:S(2)}, u32[]{:S(2)}) async-start(f32[32,8,256]{2,1,0:T(8,128)} %copy.46), calls=%async_computation.1 | async-start | bytes 524288 | tf_op jit(solution)/shard_map/all_to_all | solution.py:129
  55.7 9.8 %all-to-all-done.1 = f32[32,8,256]{2,1,0:T(8,128)S(1)} async-done(((f32[32,8,256]{2,1,0:T(8,128)}), f32[32,8,256]{2,1,0:T(8,128)S(1)}, u32[]{:S(2)}, u32[]{:S(2)}) %all-to-all-start.1) | async-done | bytes 262176 | tf_op jit(solution)/shard_map/all_to_all | solution.py:129
  65.7 42.2 %while.22 = (s32[]{:T(128)}, f32[2,128,256]{2,1,0:T(8,128)S(1)}, f32[2,128,256]{2,1,0:T(8,128)S(1)}, f32[2,128,256]{2,1,0:T(8,128)S(1)}, f32[2,1,1]{0,2,1:T(1,12...) while((s32[]{:T(128)}, f32[2,128,256]{2,1,0:T(8,128)S(1)}, ...), condition=%wide.region_1.2_spmd.clone.clone.clone, body=%wide.region_0.1_spmd.clone.clone.clone.sunk | while | flops 3704962 | bytes 17105376 | solution.py:156
  66.1 1.7 %collective-permute-start.1 = (f32[2,2,4,256]{3,2,1,0:T(4,128)S(1)}, f32[2,2,4,256]{3,2,1,0:T(4,128)S(1)}, u32[]{:S(2)}, u32[]{:S(2)}) collective-permute-start(f32[2,2,4,256]{3,2,1,0:T(4,128)S(1)} %get-tuple-element.405), channel_id=1, source_target_pairs={{0,1},{1,0},{2,3},{3,2},{4,5},{5,4},{6,7},{7,6},{8,9},{9,8},{10,11... | collective-permute-start | bytes 49160 | tf_op jit(solution)/shard_map/while/body/eval_jaxpr/ppermute | solution.py:27
  72.1 1.7 %collective-permute-start = (f32[2,2,4,256]{3,2,1,0:T(4,128)S(1)}, f32[2,2,4,256]{3,2,1,0:T(4,128)S(1)}, u32[]{:S(2)}, u32[]{:S(2)}) collective-permute-start(f32[2,2,4,256]{3,2,1,0:T(4,128)S(1)} %get-tuple-element.404), channel_id=1, source_target_pairs={{1,0},{0,1},{3,2},{2,3},{5,4},{4,5},{7,6},{6,7},{9,8},{8,9},{11,10... | collective-permute-start | bytes 49160 | tf_op jit(solution)/shard_map/while/body/eval_jaxpr/ppermute | solution.py:28
  75.9 1.7 %collective-permute-done.1 = f32[2,2,4,256]{3,2,1,0:T(4,128)S(1)} collective-permute-done((f32[2,2,4,256]{3,2,1,0:T(4,128)S(1)}, f32[2,2,4,256]{3,2,1,0:T(4,128)S(1)}, u32[]{:S(2)}, u32[]{:S(2)}) %collective-permute-start.1) | collective-permute-done | bytes 16416 | tf_op jit(solution)/shard_map/while/body/eval_jaxpr/ppermute | solution.py:27
  80.2 1.7 %collective-permute-start.1 = (f32[2,2,4,256]{3,2,1,0:T(4,128)S(1)}, f32[2,2,4,256]{3,2,1,0:T(4,128)S(1)}, u32[]{:S(2)}, u32[]{:S(2)}) collective-permute-start(f32[2,2,4,256]{3,2,1,0:T(4,128)S(1)} %get-tuple-element.405), channel_id=1, source_target_pairs={{0,1},{1,0},{2,3},{3,2},{4,5},{5,4},{6,7},{7,6},{8,9},{9,8},{10,11... | collective-permute-start | bytes 49160 | tf_op jit(solution)/shard_map/while/body/eval_jaxpr/ppermute | solution.py:27
  86.1 1.7 %collective-permute-start = (f32[2,2,4,256]{3,2,1,0:T(4,128)S(1)}, f32[2,2,4,256]{3,2,1,0:T(4,128)S(1)}, u32[]{:S(2)}, u32[]{:S(2)}) collective-permute-start(f32[2,2,4,256]{3,2,1,0:T(4,128)S(1)} %get-tuple-element.404), channel_id=1, source_target_pairs={{1,0},{0,1},{3,2},{2,3},{5,4},{4,5},{7,6},{6,7},{9,8},{8,9},{11,10... | collective-permute-start | bytes 49160 | tf_op jit(solution)/shard_map/while/body/eval_jaxpr/ppermute | solution.py:28
  89.9 1.7 %collective-permute-done.1 = f32[2,2,4,256]{3,2,1,0:T(4,128)S(1)} collective-permute-done((f32[2,2,4,256]{3,2,1,0:T(4,128)S(1)}, f32[2,2,4,256]{3,2,1,0:T(4,128)S(1)}, u32[]{:S(2)}, u32[]{:S(2)}) %collective-permute-start.1) | collective-permute-done | bytes 16416 | tf_op jit(solution)/shard_map/while/body/eval_jaxpr/ppermute | solution.py:27
  94.3 1.7 %collective-permute-start.1 = (f32[2,2,4,256]{3,2,1,0:T(4,128)S(1)}, f32[2,2,4,256]{3,2,1,0:T(4,128)S(1)}, u32[]{:S(2)}, u32[]{:S(2)}) collective-permute-start(f32[2,2,4,256]{3,2,1,0:T(4,128)S(1)} %get-tuple-element.405), channel_id=1, source_target_pairs={{0,1},{1,0},{2,3},{3,2},{4,5},{5,4},{6,7},{7,6},{8,9},{9,8},{10,11... | collective-permute-start | bytes 49160 | tf_op jit(solution)/shard_map/while/body/eval_jaxpr/ppermute | solution.py:27
  100.2 1.7 %collective-permute-start = (f32[2,2,4,256]{3,2,1,0:T(4,128)S(1)}, f32[2,2,4,256]{3,2,1,0:T(4,128)S(1)}, u32[]{:S(2)}, u32[]{:S(2)}) collective-permute-start(f32[2,2,4,256]{3,2,1,0:T(4,128)S(1)} %get-tuple-element.404), channel_id=1, source_target_pairs={{1,0},{0,1},{3,2},{2,3},{5,4},{4,5},{7,6},{6,7},{9,8},{8,9},{11,10... | collective-permute-start | bytes 49160 | tf_op jit(solution)/shard_map/while/body/eval_jaxpr/ppermute | solution.py:28
  104.0 1.7 %collective-permute-done.1 = f32[2,2,4,256]{3,2,1,0:T(4,128)S(1)} collective-permute-done((f32[2,2,4,256]{3,2,1,0:T(4,128)S(1)}, f32[2,2,4,256]{3,2,1,0:T(4,128)S(1)}, u32[]{:S(2)}, u32[]{:S(2)}) %collective-permute-start.1) | collective-permute-done | bytes 16416 | tf_op jit(solution)/shard_map/while/body/eval_jaxpr/ppermute | solution.py:27
  108.1 12.7 %all_to_all.63 = f32[2,128,256]{2,0,1:T(2,128)S(1)} all-to-all(f32[2,128,256]{2,0,1:T(2,128)S(1)} %copy.48), channel_id=1, replica_groups=mesh['tm'=16,'band'=2] {'tm'}, dimensions={1} | all-to-all | bytes 524288 | tf_op jit(solution)/shard_map/all_to_all | solution.py:157
  121.6 12.7 %all_to_all.64 = f32[32,8,256]{2,1,0:T(8,128)S(1)} all-to-all(f32[32,8,256]{2,1,0:T(8,128)S(1)} %copy.50), channel_id=1, replica_groups=mesh['tm'=16,'band'=2] {'tm'}, dimensions={0} | all-to-all | bytes 524288 | tf_op jit(solution)/shard_map/all_to_all | solution.py:158
  135.9 1.7 %collective-permute-start.12 = (f32[2,1,256]{2,1,0:T(1,128)S(1)}, f32[2,1,256]{2,1,0:T(1,128)S(1)}, u32[]{:S(2)}, u32[]{:S(2)}) collective-permute-start(f32[2,1,256]{2,1,0:T(1,128)S(1)} %get-tuple-element.266), channel_id=1, source_target_pairs={{1,0},{0,1},{3,2},{2,3},{5,4},{4,5},{7,6},{6,7},{9,8},{8,9},{11,10... | collective-permute-start | bytes 6152 | tf_op jit(solution)/shard_map/ppermute | solution.py:28
  137.5 1.6 collective-permute-done.11
  139.6 7.2 %collective-permute-done.13 = f32[1,128,256]{2,1,0:T(8,128)S(1)} collective-permute-done((f32[1,128,256]{2,1,0:T(8,128)S(1)}, f32[1,128,256]{2,1,0:T(8,128)S(1)}, u32[]{:S(2)}, u32[]{:S(2)}) %collective-permute-start.13) | collective-permute-done | bytes 131104 | tf_op jit(solution)/shard_map/ppermute | solution.py:35
  147.0 2.5 %collective-permute-done.14 = f32[1,128,256]{2,1,0:T(8,128)S(1)} collective-permute-done((f32[1,128,256]{2,1,0:T(8,128)S(1)}, f32[1,128,256]{2,1,0:T(8,128)S(1)}, u32[]{:S(2)}, u32[]{:S(2)}) %collective-permute-start.14) | collective-permute-done | bytes 131104 | tf_op jit(solution)/shard_map/ppermute | solution.py:35
  149.5 1.7 %collective-permute-start.15 = (f32[2,1,256]{2,1,0:T(1,128)S(1)}, f32[2,1,256]{2,1,0:T(1,128)S(1)}, u32[]{:S(2)}, u32[]{:S(2)}) collective-permute-start(f32[2,1,256]{2,1,0:T(1,128)S(1)} %get-tuple-element.259), channel_id=1, source_target_pairs={{0,1},{1,0},{2,3},{3,2},{4,5},{5,4},{6,7},{7,6},{8,9},{9,8},{10,11... | collective-permute-start | bytes 6152 | tf_op jit(solution)/shard_map/ppermute | solution.py:27
  151.6 1.6 collective-permute-done.15
  153.1 1.7 %collective-permute-done.16 = f32[2,1,256]{2,1,0:T(1,128)S(1)} collective-permute-done((f32[2,1,256]{2,1,0:T(1,128)S(1)}, f32[2,1,256]{2,1,0:T(1,128)S(1)}, u32[]{:S(2)}, u32[]{:S(2)}) %collective-permute-start.16) | collective-permute-done | bytes 2080 | tf_op jit(solution)/shard_map/ppermute | solution.py:28
  (245 shorter events, 43.0 us)
Async XLA Ops:
  1.3 8.5 %copy-start.3 = (s32[2,128,256]{2,1,0:T(8,128)S(1)}, s32[2,128,256]{2,1,0:T(8,128)}, u32[]{:S(2)}) copy-start(s32[2,128,256]{2,1,0:T(8,128)} %param.11) | copy-start | bytes 786436
  1.3 9.1 %collective-permute-start.2 = (s32[1,256]{1,0:T(1,128)S(1)}, s32[1,256]{1,0:T(1,128)S(1)}, u32[]{:S(2)}, u32[]{:S(2)}) collective-permute-start(s32[1,256]{1,0:T(1,128)S(1)} %slice_bitcast_fusion.4), channel_id=1, source_target_pairs={{0,1},{1,0},{2,3},{3,2},{4,5},{5,4},{6,7},{7,6},{8,9},{9,8},{10,11... | collective-permute-start | bytes 3080 | tf_op jit(solution)/shard_map/ppermute | solution.py:35
  5.3 7.2 %collective-permute-start.3 = (f32[1,128,256]{2,1,0:T(8,128)S(1)}, f32[1,128,256]{2,1,0:T(8,128)S(1)}, u32[]{:S(2)}, u32[]{:S(2)}) collective-permute-start(f32[1,128,256]{2,1,0:T(8,128)S(1)} %get-tuple-element.313), channel_id=1, source_target_pairs={{0,2},{2,4},{4,6},{6,8},{8,10},{10,12},{12,14},{14,16},{16,18},{18... | collective-permute-start | bytes 393224 | tf_op jit(solution)/shard_map/ppermute | solution.py:27
  5.4 7.2 %collective-permute-start.4 = (f32[1,128,256]{2,1,0:T(8,128)S(1)}, f32[1,128,256]{2,1,0:T(8,128)S(1)}, u32[]{:S(2)}, u32[]{:S(2)}) collective-permute-start(f32[1,128,256]{2,1,0:T(8,128)S(1)} %get-tuple-element.314), channel_id=1, source_target_pairs={{2,0},{4,2},{6,4},{8,6},{10,8},{12,10},{14,12},{16,14},{18,16},{20... | collective-permute-start | bytes 393224 | tf_op jit(solution)/shard_map/ppermute | solution.py:28
  10.4 2.1 %copy-start = (f32[2,128,256]{2,1,0:T(8,128)S(1)}, f32[2,128,256]{2,1,0:T(8,128)}, u32[]{:S(2)}) copy-start(f32[2,128,256]{2,1,0:T(8,128)} %param.7) | copy-start | bytes 786436
  13.6 3.7 %collective-permute-start.5 = (f32[2,1,256]{2,1,0:T(1,128)S(1)}, f32[2,1,256]{2,1,0:T(1,128)S(1)}, u32[]{:S(2)}, u32[]{:S(2)}) collective-permute-start(f32[2,1,256]{2,1,0:T(1,128)S(1)} %get-tuple-element.297), channel_id=1, source_target_pairs={{0,1},{1,0},{2,3},{3,2},{4,5},{5,4},{6,7},{7,6},{8,9},{9,8},{10,11... | collective-permute-start | bytes 6152 | tf_op jit(solution)/shard_map/ppermute | solution.py:27
  13.7 3.6 %collective-permute-start.6 = (f32[2,1,256]{2,1,0:T(1,128)S(1)}, f32[2,1,256]{2,1,0:T(1,128)S(1)}, u32[]{:S(2)}, u32[]{:S(2)}) collective-permute-start(f32[2,1,256]{2,1,0:T(1,128)S(1)} %get-tuple-element.298), channel_id=1, source_target_pairs={{1,0},{0,1},{3,2},{2,3},{5,4},{4,5},{7,6},{6,7},{9,8},{8,9},{11,10... | collective-permute-start | bytes 6152 | tf_op jit(solution)/shard_map/ppermute | solution.py:28
  17.4 7.2 %collective-permute-start.7 = (f32[1,128,256]{2,1,0:T(8,128)S(1)}, f32[1,128,256]{2,1,0:T(8,128)S(1)}, u32[]{:S(2)}, u32[]{:S(2)}) collective-permute-start(f32[1,128,256]{2,1,0:T(8,128)S(1)} %get-tuple-element.295), channel_id=1, source_target_pairs={{0,2},{2,4},{4,6},{6,8},{8,10},{10,12},{12,14},{14,16},{16,18},{18... | collective-permute-start | bytes 393224 | tf_op jit(solution)/shard_map/ppermute | solution.py:35
  24.7 2.6 %collective-permute-start.8 = (f32[1,128,256]{2,1,0:T(8,128)S(1)}, f32[1,128,256]{2,1,0:T(8,128)S(1)}, u32[]{:S(2)}, u32[]{:S(2)}) collective-permute-start(f32[1,128,256]{2,1,0:T(8,128)S(1)} %get-tuple-element.294), channel_id=1, source_target_pairs={{0,30},{2,0},{4,2},{6,4},{8,6},{10,8},{12,10},{14,12},{16,14},{18,... | collective-permute-start | bytes 393224 | tf_op jit(solution)/shard_map/ppermute | solution.py:35
  27.3 3.7 %collective-permute-start.9 = (f32[2,1,256]{2,1,0:T(1,128)S(1)}, f32[2,1,256]{2,1,0:T(1,128)S(1)}, u32[]{:S(2)}, u32[]{:S(2)}) collective-permute-start(f32[2,1,256]{2,1,0:T(1,128)S(1)} %get-tuple-element.291), channel_id=1, source_target_pairs={{0,1},{1,0},{2,3},{3,2},{4,5},{5,4},{6,7},{7,6},{8,9},{9,8},{10,11... | collective-permute-start | bytes 6152 | tf_op jit(solution)/shard_map/ppermute | solution.py:27
  29.4 3.6 %collective-permute-start.10 = (f32[2,1,256]{2,1,0:T(1,128)S(1)}, f32[2,1,256]{2,1,0:T(1,128)S(1)}, u32[]{:S(2)}, u32[]{:S(2)}) collective-permute-start(f32[2,1,256]{2,1,0:T(1,128)S(1)} %get-tuple-element.292), channel_id=1, source_target_pairs={{1,0},{0,1},{3,2},{2,3},{5,4},{4,5},{7,6},{6,7},{9,8},{8,9},{11,10... | collective-permute-start | bytes 6152 | tf_op jit(solution)/shard_map/ppermute | solution.py:28
  35.9 14.5 %all-to-all-start = ((f32[2,128,256]{2,0,1:T(2,128)}), f32[2,128,256]{2,0,1:T(2,128)S(1)}, u32[]{:S(2)}, u32[]{:S(2)}) async-start(f32[2,128,256]{2,0,1:T(2,128)} %copy.43), calls=%async_computation | async-start | bytes 524288 | tf_op jit(solution)/shard_map/all_to_all | solution.py:128
  52.0 13.5 %all-to-all-start.1 = ((f32[32,8,256]{2,1,0:T(8,128)}), f32[32,8,256]{2,1,0:T(8,128)S(1)}, u32[]{:S(2)}, u32[]{:S(2)}) async-start(f32[32,8,256]{2,1,0:T(8,128)} %copy.46), calls=%async_computation.1 | async-start | bytes 524288 | tf_op jit(solution)/shard_map/all_to_all | solution.py:129
  65.7 3.8 %collective-permute-start = (f32[2,2,4,256]{3,2,1,0:T(4,128)S(1)}, f32[2,2,4,256]{3,2,1,0:T(4,128)S(1)}, u32[]{:S(2)}, u32[]{:S(2)}) collective-permute-start(f32[2,2,4,256]{3,2,1,0:T(4,128)S(1)} %get-tuple-element.404), channel_id=1, source_target_pairs={{1,0},{0,1},{3,2},{2,3},{5,4},{4,5},{7,6},{6,7},{9,8},{8,9},{11,10... | collective-permute-start | bytes 49160 | tf_op jit(solution)/shard_map/while/body/eval_jaxpr/ppermute | solution.py:28
  66.1 3.7 %collective-permute-start.1 = (f32[2,2,4,256]{3,2,1,0:T(4,128)S(1)}, f32[2,2,4,256]{3,2,1,0:T(4,128)S(1)}, u32[]{:S(2)}, u32[]{:S(2)}) collective-permute-start(f32[2,2,4,256]{3,2,1,0:T(4,128)S(1)} %get-tuple-element.405), channel_id=1, source_target_pairs={{0,1},{1,0},{2,3},{3,2},{4,5},{5,4},{6,7},{7,6},{8,9},{9,8},{10,11... | collective-permute-start | bytes 49160 | tf_op jit(solution)/shard_map/while/body/eval_jaxpr/ppermute | solution.py:27
  72.1 3.8 %collective-permute-start = (f32[2,2,4,256]{3,2,1,0:T(4,128)S(1)}, f32[2,2,4,256]{3,2,1,0:T(4,128)S(1)}, u32[]{:S(2)}, u32[]{:S(2)}) collective-permute-start(f32[2,2,4,256]{3,2,1,0:T(4,128)S(1)} %get-tuple-element.404), channel_id=1, source_target_pairs={{1,0},{0,1},{3,2},{2,3},{5,4},{4,5},{7,6},{6,7},{9,8},{8,9},{11,10... | collective-permute-start | bytes 49160 | tf_op jit(solution)/shard_map/while/body/eval_jaxpr/ppermute | solution.py:28
  73.8 3.7 %collective-permute-start.1 = (f32[2,2,4,256]{3,2,1,0:T(4,128)S(1)}, f32[2,2,4,256]{3,2,1,0:T(4,128)S(1)}, u32[]{:S(2)}, u32[]{:S(2)}) collective-permute-start(f32[2,2,4,256]{3,2,1,0:T(4,128)S(1)} %get-tuple-element.405), channel_id=1, source_target_pairs={{0,1},{1,0},{2,3},{3,2},{4,5},{5,4},{6,7},{7,6},{8,9},{9,8},{10,11... | collective-permute-start | bytes 49160 | tf_op jit(solution)/shard_map/while/body/eval_jaxpr/ppermute | solution.py:27
  79.8 3.8 %collective-permute-start = (f32[2,2,4,256]{3,2,1,0:T(4,128)S(1)}, f32[2,2,4,256]{3,2,1,0:T(4,128)S(1)}, u32[]{:S(2)}, u32[]{:S(2)}) collective-permute-start(f32[2,2,4,256]{3,2,1,0:T(4,128)S(1)} %get-tuple-element.404), channel_id=1, source_target_pairs={{1,0},{0,1},{3,2},{2,3},{5,4},{4,5},{7,6},{6,7},{9,8},{8,9},{11,10... | collective-permute-start | bytes 49160 | tf_op jit(solution)/shard_map/while/body/eval_jaxpr/ppermute | solution.py:28
  80.2 3.7 %collective-permute-start.1 = (f32[2,2,4,256]{3,2,1,0:T(4,128)S(1)}, f32[2,2,4,256]{3,2,1,0:T(4,128)S(1)}, u32[]{:S(2)}, u32[]{:S(2)}) collective-permute-start(f32[2,2,4,256]{3,2,1,0:T(4,128)S(1)} %get-tuple-element.405), channel_id=1, source_target_pairs={{0,1},{1,0},{2,3},{3,2},{4,5},{5,4},{6,7},{7,6},{8,9},{9,8},{10,11... | collective-permute-start | bytes 49160 | tf_op jit(solution)/shard_map/while/body/eval_jaxpr/ppermute | solution.py:27
  86.1 3.8 %collective-permute-start = (f32[2,2,4,256]{3,2,1,0:T(4,128)S(1)}, f32[2,2,4,256]{3,2,1,0:T(4,128)S(1)}, u32[]{:S(2)}, u32[]{:S(2)}) collective-permute-start(f32[2,2,4,256]{3,2,1,0:T(4,128)S(1)} %get-tuple-element.404), channel_id=1, source_target_pairs={{1,0},{0,1},{3,2},{2,3},{5,4},{4,5},{7,6},{6,7},{9,8},{8,9},{11,10... | collective-permute-start | bytes 49160 | tf_op jit(solution)/shard_map/while/body/eval_jaxpr/ppermute | solution.py:28
  87.9 3.7 %collective-permute-start.1 = (f32[2,2,4,256]{3,2,1,0:T(4,128)S(1)}, f32[2,2,4,256]{3,2,1,0:T(4,128)S(1)}, u32[]{:S(2)}, u32[]{:S(2)}) collective-permute-start(f32[2,2,4,256]{3,2,1,0:T(4,128)S(1)} %get-tuple-element.405), channel_id=1, source_target_pairs={{0,1},{1,0},{2,3},{3,2},{4,5},{5,4},{6,7},{7,6},{8,9},{9,8},{10,11... | collective-permute-start | bytes 49160 | tf_op jit(solution)/shard_map/while/body/eval_jaxpr/ppermute | solution.py:27
  93.8 3.8 %collective-permute-start = (f32[2,2,4,256]{3,2,1,0:T(4,128)S(1)}, f32[2,2,4,256]{3,2,1,0:T(4,128)S(1)}, u32[]{:S(2)}, u32[]{:S(2)}) collective-permute-start(f32[2,2,4,256]{3,2,1,0:T(4,128)S(1)} %get-tuple-element.404), channel_id=1, source_target_pairs={{1,0},{0,1},{3,2},{2,3},{5,4},{4,5},{7,6},{6,7},{9,8},{8,9},{11,10... | collective-permute-start | bytes 49160 | tf_op jit(solution)/shard_map/while/body/eval_jaxpr/ppermute | solution.py:28
  94.3 3.7 %collective-permute-start.1 = (f32[2,2,4,256]{3,2,1,0:T(4,128)S(1)}, f32[2,2,4,256]{3,2,1,0:T(4,128)S(1)}, u32[]{:S(2)}, u32[]{:S(2)}) collective-permute-start(f32[2,2,4,256]{3,2,1,0:T(4,128)S(1)} %get-tuple-element.405), channel_id=1, source_target_pairs={{0,1},{1,0},{2,3},{3,2},{4,5},{5,4},{6,7},{7,6},{8,9},{9,8},{10,11... | collective-permute-start | bytes 49160 | tf_op jit(solution)/shard_map/while/body/eval_jaxpr/ppermute | solution.py:27
  100.2 3.8 %collective-permute-start = (f32[2,2,4,256]{3,2,1,0:T(4,128)S(1)}, f32[2,2,4,256]{3,2,1,0:T(4,128)S(1)}, u32[]{:S(2)}, u32[]{:S(2)}) collective-permute-start(f32[2,2,4,256]{3,2,1,0:T(4,128)S(1)} %get-tuple-element.404), channel_id=1, source_target_pairs={{1,0},{0,1},{3,2},{2,3},{5,4},{4,5},{7,6},{6,7},{9,8},{8,9},{11,10... | collective-permute-start | bytes 49160 | tf_op jit(solution)/shard_map/while/body/eval_jaxpr/ppermute | solution.py:28
  101.9 3.7 %collective-permute-start.1 = (f32[2,2,4,256]{3,2,1,0:T(4,128)S(1)}, f32[2,2,4,256]{3,2,1,0:T(4,128)S(1)}, u32[]{:S(2)}, u32[]{:S(2)}) collective-permute-start(f32[2,2,4,256]{3,2,1,0:T(4,128)S(1)} %get-tuple-element.405), channel_id=1, source_target_pairs={{0,1},{1,0},{2,3},{3,2},{4,5},{5,4},{6,7},{7,6},{8,9},{9,8},{10,11... | collective-permute-start | bytes 49160 | tf_op jit(solution)/shard_map/while/body/eval_jaxpr/ppermute | solution.py:27
  134.4 21.3 %copy-start.2 = (f32[2,128,256]{2,1,0:T(8,128)}, f32[2,128,256]{2,1,0:T(8,128)S(1)}, u32[]{:S(2)}) copy-start(f32[2,128,256]{2,1,0:T(8,128)S(1)} %get-tuple-element.207) | copy-start | bytes 786436
  135.4 3.7 %collective-permute-start.11 = (f32[2,1,256]{2,1,0:T(1,128)S(1)}, f32[2,1,256]{2,1,0:T(1,128)S(1)}, u32[]{:S(2)}, u32[]{:S(2)}) collective-permute-start(f32[2,1,256]{2,1,0:T(1,128)S(1)} %get-tuple-element.265), channel_id=1, source_target_pairs={{0,1},{1,0},{2,3},{3,2},{4,5},{5,4},{6,7},{7,6},{8,9},{9,8},{10,11... | collective-permute-start | bytes 6152 | tf_op jit(solution)/shard_map/ppermute | solution.py:27
  135.9 3.6 %collective-permute-start.12 = (f32[2,1,256]{2,1,0:T(1,128)S(1)}, f32[2,1,256]{2,1,0:T(1,128)S(1)}, u32[]{:S(2)}, u32[]{:S(2)}) collective-permute-start(f32[2,1,256]{2,1,0:T(1,128)S(1)} %get-tuple-element.266), channel_id=1, source_target_pairs={{1,0},{0,1},{3,2},{2,3},{5,4},{4,5},{7,6},{6,7},{9,8},{8,9},{11,10... | collective-permute-start | bytes 6152 | tf_op jit(solution)/shard_map/ppermute | solution.py:28
  139.6 7.2 %collective-permute-start.13 = (f32[1,128,256]{2,1,0:T(8,128)S(1)}, f32[1,128,256]{2,1,0:T(8,128)S(1)}, u32[]{:S(2)}, u32[]{:S(2)}) collective-permute-start(f32[1,128,256]{2,1,0:T(8,128)S(1)} %get-tuple-element.263), channel_id=1, source_target_pairs={{0,2},{2,4},{4,6},{6,8},{8,10},{10,12},{12,14},{14,16},{16,18},{18... | collective-permute-start | bytes 393224 | tf_op jit(solution)/shard_map/ppermute | solution.py:35
  146.9 2.6 %collective-permute-start.14 = (f32[1,128,256]{2,1,0:T(8,128)S(1)}, f32[1,128,256]{2,1,0:T(8,128)S(1)}, u32[]{:S(2)}, u32[]{:S(2)}) collective-permute-start(f32[1,128,256]{2,1,0:T(8,128)S(1)} %get-tuple-element.262), channel_id=1, source_target_pairs={{0,30},{2,0},{4,2},{6,4},{8,6},{10,8},{12,10},{14,12},{16,14},{18,... | collective-permute-start | bytes 393224 | tf_op jit(solution)/shard_map/ppermute | solution.py:35
  149.5 3.7 %collective-permute-start.15 = (f32[2,1,256]{2,1,0:T(1,128)S(1)}, f32[2,1,256]{2,1,0:T(1,128)S(1)}, u32[]{:S(2)}, u32[]{:S(2)}) collective-permute-start(f32[2,1,256]{2,1,0:T(1,128)S(1)} %get-tuple-element.259), channel_id=1, source_target_pairs={{0,1},{1,0},{2,3},{3,2},{4,5},{5,4},{6,7},{7,6},{8,9},{9,8},{10,11... | collective-permute-start | bytes 6152 | tf_op jit(solution)/shard_map/ppermute | solution.py:27
  151.2 3.6 %collective-permute-start.16 = (f32[2,1,256]{2,1,0:T(1,128)S(1)}, f32[2,1,256]{2,1,0:T(1,128)S(1)}, u32[]{:S(2)}, u32[]{:S(2)}) collective-permute-start(f32[2,1,256]{2,1,0:T(1,128)S(1)} %get-tuple-element.260), channel_id=1, source_target_pairs={{1,0},{0,1},{3,2},{2,3},{5,4},{4,5},{7,6},{6,7},{9,8},{8,9},{11,10... | collective-permute-start | bytes 6152 | tf_op jit(solution)/shard_map/ppermute | solution.py:28
  (3 other events, 4.0 us)
where the time goes:
time: 158 us
  waiting for transfers between devices  66.5 us (42%)
  starting transfers between devices  36.7 us (23%)
  blocking collectives  25.4 us (16%)
  local copies, waits for them, and re-layouts  14.2 us (9%)
  other arithmetic  11.9 us (8%)
    ppermute x5, waiting for transfers between devices, passed_along(): lax.ppermute(value, axis, [(i, (i + by) % size) for i in range(size)])  19.3 us
    ppermute x11, starting transfers between devices, extended(): after = lax.ppermute(leading, axis, down)  15 us
    ppermute x11, waiting for transfers between devices, extended(): before = lax.ppermute(last, axis, up)  13.9 us
    ppermute x11, waiting for transfers between devices, extended(): after = lax.ppermute(leading, axis, down)  13.4 us
    all_to_all x1, blocking collectives, shards(): lax.all_to_all(accum, 'tm', split_axis=1, concat_axis=0, tiled=True)  12.7 us
    all_to_all x1, blocking collectives, shards(): lax.all_to_all(mixed_back, 'tm', split_axis=0, concat_axis=1, tiled=True)  12.7 us
    ppermute x11, starting transfers between devices, extended(): before = lax.ppermute(last, axis, up)  10.4 us
    all_to_all x1, waiting for transfers between devices, shards(): lax.all_to_all(residual, 'tm', split_axis=1, concat_axis=0, tiled=True)  9.98 us
  transfers between devices with their start and end apart: 29, of which 27 were waited for; matrix products, arithmetic and copies ran while one was open for 2% of the time, Pallas kernels for 0%

commit v1 on v0

--- a/solution.py
+++ b/solution.py
@@ -15,6 +15,22 @@
 cheb_slope = 0.5
 half_width = 4.0
 deep_width = 4
+
+
+def pairwise_exchange(value, axis, split, join):
+    ways, here = (lax.axis_size(axis), lax.axis_index(axis))
+    width = value.shape[split] // ways
+    lengths = list(value.shape)
+    lengths[split] = width
+    height = lengths[join]
+    lengths[join] = height * ways
+    full = jnp.zeros(lengths, value.dtype)
+    for mask in range(ways):
+        part = lax.dynamic_slice_in_dim(value, (here ^ mask) * width, width, axis=split)
+        if mask:
+            part = lax.ppermute(part, axis, [(d, d ^ mask) for d in range(ways)])
+        full = lax.dynamic_update_slice_in_dim(full, part, (here ^ mask) * height, axis=join)
+    return full
 
 
 def extended(value, sides, width):
@@ -154,7 +170,7 @@
         return (accum, rem_wide, dir_wide, weight_now)
 
     accum = lax.fori_loop(0, ORDER // deep_width, sweep_block, start)[0]
-    mixed_back = to_slices(lax.all_to_all(accum, "tm", split_axis=1, concat_axis=0, tiled=True))
+    mixed_back = to_slices(pairwise_exchange(accum, "tm", 1, 0))
     timed = lax.all_to_all(mixed_back, "tm", split_axis=0, concat_axis=1, tiled=True)
     solution = guess + relaxation * timed
     propagated = apply_pairs(expo * solution, (0, 1, 2, 3))

time: 158 us -> 171 us (1.082)
  starting transfers between devices: 36.7 us -> 58 us
  blocking collectives: 25.4 us -> 14.4 us
  waiting for transfers between devices: 66.5 us -> 68.4 us
    ppermute x0 -> x15, starting transfers between devices: none -> 21.1 us  [pairwise_exchange(): part = lax.ppermute(part, axis, [(d, d ^ mask) for d in range(ways)])]
    all_to_all x1 -> x0, blocking collectives: 12.7 us -> none  [shards(): lax.all_to_all(accum, 'tm', split_axis=1, concat_axis=0, tiled=True)]
    ppermute x11, waiting for transfers between devices: 13.9 us -> 10.9 us  [extended(): before = lax.ppermute(last, axis, up)]
    ppermute x0 -> x15, waiting for transfers between devices: none -> 2.76 us  [pairwise_exchange(): part = lax.ppermute(part, axis, [(d, d ^ mask) for d in range(ways)])]
    ppermute x11, starting transfers between devices: 10.4 us -> 12.6 us  [extended(): before = lax.ppermute(last, axis, up)]
    all_to_all x1, blocking collectives: 12.7 us -> 14.4 us  [shards(): lax.all_to_all(mixed_back, 'tm', split_axis=0, concat_axis=1, tiled=True)]
  transfers between devices with their start and end apart: 29 -> 44, of which waited for: 27 -> 29; matrix products, arithmetic and copies ran while one was open for 2% -> 1% of each run, Pallas kernels for 0% -> 0%
where the time goes in v1:
time: 171 us; the launch traced here: 170 us
  waiting for transfers between devices  68.4 us (40%)
  starting transfers between devices  58 us (34%)
  blocking collectives  14.4 us (8%)
  local copies, waits for them, and re-layouts  14.2 us (8%)
  other arithmetic  11.9 us (7%)
    ppermute x15, starting transfers between devices, pairwise_exchange(): part = lax.ppermute(part, axis, [(d, d ^ mask) for d in range(ways)])  21.1 us
    ppermute x5, waiting for transfers between devices, passed_along(): lax.ppermute(value, axis, [(i, (i + by) % size) for i in range(size)])  20.4 us
    ppermute x11, waiting for transfers between devices, extended(): after = lax.ppermute(leading, axis, down)  14.7 us
    all_to_all x1, blocking collectives, shards(): lax.all_to_all(mixed_back, 'tm', split_axis=0, concat_axis=1, tiled=True)  14.4 us
    ppermute x11, starting transfers between devices, extended(): after = lax.ppermute(leading, axis, down)  13.9 us
    ppermute x11, starting transfers between devices, extended(): before = lax.ppermute(last, axis, up)  12.6 us
    ppermute x11, waiting for transfers between devices, extended(): before = lax.ppermute(last, axis, up)  10.9 us
    all_to_all x1, waiting for transfers between devices, shards(): lax.all_to_all(residual, 'tm', split_axis=1, concat_axis=0, tiled=True)  9.98 us
  transfers between devices with their start and end apart: 44, of which 29 were waited for; matrix products, arithmetic and copies ran while one was open for 1% of the time, Pallas kernels for 0%

profile of v1, /device:TPU:0, one launch (start us, length us, event | category | flops | bytes accessed | tf_op | source)
XLA Modules:
  0.0 170.2 jit_solution(246182008078574686)
XLA Ops:
  2.2 5.0 %collective-permute-start.4 = (f32[1,128,256]{2,1,0:T(8,128)S(1)}, f32[1,128,256]{2,1,0:T(8,128)S(1)}, u32[]{:S(2)}, u32[]{:S(2)}) collective-permute-start(f32[1,128,256]{2,1,0:T(8,128)S(1)} %get-tuple-element.330), channel_id=1, source_target_pairs={{2,0},{4,2},{6,4},{8,6},{10,8},{12,10},{14,12},{16,14},{18,16},{20... | collective-permute-start | bytes 393224 | tf_op jit(solution)/shard_map/ppermute | solution.py:44
  7.3 1.9 %collective-permute-start.2 = (s32[1,256]{1,0:T(1,128)S(1)}, s32[1,256]{1,0:T(1,128)S(1)}, u32[]{:S(2)}, u32[]{:S(2)}) collective-permute-start(s32[1,256]{1,0:T(1,128)S(1)} %slice_bitcast_fusion.4), channel_id=1, source_target_pairs={{0,1},{1,0},{2,3},{3,2},{4,5},{5,4},{6,7},{7,6},{8,9},{9,8},{10,11... | collective-permute-start | bytes 3080 | tf_op jit(solution)/shard_map/ppermute | solution.py:51
  12.9 1.9 %collective-permute-start.5 = (f32[2,1,256]{2,1,0:T(1,128)S(1)}, f32[2,1,256]{2,1,0:T(1,128)S(1)}, u32[]{:S(2)}, u32[]{:S(2)}) collective-permute-start(f32[2,1,256]{2,1,0:T(1,128)S(1)} %get-tuple-element.313), channel_id=1, source_target_pairs={{0,1},{1,0},{2,3},{3,2},{4,5},{5,4},{6,7},{7,6},{8,9},{9,8},{10,11... | collective-permute-start | bytes 6152 | tf_op jit(solution)/shard_map/ppermute | solution.py:43
  16.6 1.9 %collective-permute-done.6 = f32[2,1,256]{2,1,0:T(1,128)S(1)} collective-permute-done((f32[2,1,256]{2,1,0:T(1,128)S(1)}, f32[2,1,256]{2,1,0:T(1,128)S(1)}, u32[]{:S(2)}, u32[]{:S(2)}) %collective-permute-start.6) | collective-permute-done | bytes 2080 | tf_op jit(solution)/shard_map/ppermute | solution.py:44
  18.6 7.2 %collective-permute-done.7 = f32[1,128,256]{2,1,0:T(8,128)S(1)} collective-permute-done((f32[1,128,256]{2,1,0:T(8,128)S(1)}, f32[1,128,256]{2,1,0:T(8,128)S(1)}, u32[]{:S(2)}, u32[]{:S(2)}) %collective-permute-start.7) | collective-permute-done | bytes 131104 | tf_op jit(solution)/shard_map/ppermute | solution.py:51
  26.0 2.5 %collective-permute-done.8 = f32[1,128,256]{2,1,0:T(8,128)S(1)} collective-permute-done((f32[1,128,256]{2,1,0:T(8,128)S(1)}, f32[1,128,256]{2,1,0:T(8,128)S(1)}, u32[]{:S(2)}, u32[]{:S(2)}) %collective-permute-start.8) | collective-permute-done | bytes 131104 | tf_op jit(solution)/shard_map/ppermute | solution.py:51
  28.7 1.9 %collective-permute-start.9 = (f32[2,1,256]{2,1,0:T(1,128)S(1)}, f32[2,1,256]{2,1,0:T(1,128)S(1)}, u32[]{:S(2)}, u32[]{:S(2)}) collective-permute-start(f32[2,1,256]{2,1,0:T(1,128)S(1)} %get-tuple-element.307), channel_id=1, source_target_pairs={{0,1},{1,0},{2,3},{3,2},{4,5},{5,4},{6,7},{7,6},{8,9},{9,8},{10,11... | collective-permute-start | bytes 6152 | tf_op jit(solution)/shard_map/ppermute | solution.py:43
  35.3 4.7 %all-to-all-start = ((f32[2,128,256]{2,0,1:T(2,128)}), f32[2,128,256]{2,0,1:T(2,128)S(1)}, u32[]{:S(2)}, u32[]{:S(2)}) async-start(f32[2,128,256]{2,0,1:T(2,128)} %copy.87), calls=%async_computation | async-start | bytes 524288 | tf_op jit(solution)/shard_map/all_to_all | solution.py:144
  40.0 10.0 %all-to-all-done = f32[2,128,256]{2,0,1:T(2,128)S(1)} async-done(((f32[2,128,256]{2,0,1:T(2,128)}), f32[2,128,256]{2,0,1:T(2,128)S(1)}, u32[]{:S(2)}, u32[]{:S(2)}) %all-to-all-start) | async-done | bytes 262176 | tf_op jit(solution)/shard_map/all_to_all | solution.py:144
  51.6 3.5 %all-to-all-start.1 = ((f32[32,8,256]{2,1,0:T(8,128)}), f32[32,8,256]{2,1,0:T(8,128)S(1)}, u32[]{:S(2)}, u32[]{:S(2)}) async-start(f32[32,8,256]{2,1,0:T(8,128)} %copy.90), calls=%async_computation.1 | async-start | bytes 524288 | tf_op jit(solution)/shard_map/all_to_all | solution.py:145
  55.5 9.6 %all-to-all-done.1 = f32[32,8,256]{2,1,0:T(8,128)S(1)} async-done(((f32[32,8,256]{2,1,0:T(8,128)}), f32[32,8,256]{2,1,0:T(8,128)S(1)}, u32[]{:S(2)}, u32[]{:S(2)}) %all-to-all-start.1) | async-done | bytes 262176 | tf_op jit(solution)/shard_map/all_to_all | solution.py:145
  65.2 42.2 %while.22 = (s32[]{:T(128)}, f32[2,128,256]{2,1,0:T(8,128)S(1)}, f32[2,128,256]{2,1,0:T(8,128)S(1)}, f32[2,128,256]{2,1,0:T(8,128)S(1)}, f32[2,1,1]{0,2,1:T(1,12...) while((s32[]{:T(128)}, f32[2,128,256]{2,1,0:T(8,128)S(1)}, ...), condition=%wide.region_1.2_spmd.clone.clone.clone, body=%wide.region_0.1_spmd.clone.clone.clone.sunk | while | flops 3704962 | bytes 17105376 | solution.py:172
  65.3 1.7 %collective-permute-start = (f32[2,2,4,256]{3,2,1,0:T(4,128)S(1)}, f32[2,2,4,256]{3,2,1,0:T(4,128)S(1)}, u32[]{:S(2)}, u32[]{:S(2)}) collective-permute-start(f32[2,2,4,256]{3,2,1,0:T(4,128)S(1)} %get-tuple-element.420), channel_id=1, source_target_pairs={{1,0},{0,1},{3,2},{2,3},{5,4},{4,5},{7,6},{6,7},{9,8},{8,9},{11,10... | collective-permute-start | bytes 49160 | tf_op jit(solution)/shard_map/while/body/eval_jaxpr/ppermute | solution.py:44
  69.1 1.7 collective-permute-done.1
  73.4 1.7 collective-permute-start.1
  79.3 1.7 %collective-permute-start = (f32[2,2,4,256]{3,2,1,0:T(4,128)S(1)}, f32[2,2,4,256]{3,2,1,0:T(4,128)S(1)}, u32[]{:S(2)}, u32[]{:S(2)}) collective-permute-start(f32[2,2,4,256]{3,2,1,0:T(4,128)S(1)} %get-tuple-element.420), channel_id=1, source_target_pairs={{1,0},{0,1},{3,2},{2,3},{5,4},{4,5},{7,6},{6,7},{9,8},{8,9},{11,10... | collective-permute-start | bytes 49160 | tf_op jit(solution)/shard_map/while/body/eval_jaxpr/ppermute | solution.py:44
  83.1 1.7 collective-permute-done.1
  87.4 1.7 collective-permute-start.1
  93.4 1.7 %collective-permute-start = (f32[2,2,4,256]{3,2,1,0:T(4,128)S(1)}, f32[2,2,4,256]{3,2,1,0:T(4,128)S(1)}, u32[]{:S(2)}, u32[]{:S(2)}) collective-permute-start(f32[2,2,4,256]{3,2,1,0:T(4,128)S(1)} %get-tuple-element.420), channel_id=1, source_target_pairs={{1,0},{0,1},{3,2},{2,3},{5,4},{4,5},{7,6},{6,7},{9,8},{8,9},{11,10... | collective-permute-start | bytes 49160 | tf_op jit(solution)/shard_map/while/body/eval_jaxpr/ppermute | solution.py:44
  97.2 1.7 collective-permute-done.1
  101.5 1.7 collective-permute-start.1
  107.7 1.8 %collective-permute-start.13 = (f32[2,8,256]{2,1,0:T(8,128)S(1)}, f32[2,8,256]{2,1,0:T(8,128)S(1)}, u32[]{:S(2)}, u32[]{:S(2)}) collective-permute-start(f32[2,8,256]{2,1,0:T(8,128)S(1)} %get-tuple-element.289), channel_id=1, source_target_pairs={{0,6},{2,4},{4,2},{6,0},{8,14},{10,12},{12,10},{14,8},{16,22},{18,... | collective-permute-start | bytes 49160 | tf_op jit(solution)/shard_map/ppermute | solution.py:31
  109.5 1.7 %collective-permute-start.15 = (f32[2,8,256]{2,1,0:T(8,128)S(1)}, f32[2,8,256]{2,1,0:T(8,128)S(1)}, u32[]{:S(2)}, u32[]{:S(2)}) collective-permute-start(f32[2,8,256]{2,1,0:T(8,128)S(1)} %get-tuple-element.287), channel_id=1, source_target_pairs={{0,10},{2,8},{4,14},{6,12},{8,2},{10,0},{12,6},{14,4},{16,26},{18,... | collective-permute-start | bytes 49160 | tf_op jit(solution)/shard_map/ppermute | solution.py:31
  111.8 2.2 %collective-permute-start.17 = (f32[2,8,256]{2,1,0:T(8,128)S(1)}, f32[2,8,256]{2,1,0:T(8,128)S(1)}, u32[]{:S(2)}, u32[]{:S(2)}) collective-permute-start(f32[2,8,256]{2,1,0:T(8,128)S(1)} %get-tuple-element.285), channel_id=1, source_target_pairs={{0,14},{2,12},{4,10},{6,8},{8,6},{10,4},{12,2},{14,0},{16,30},{18,... | collective-permute-start | bytes 49160 | tf_op jit(solution)/shard_map/ppermute | solution.py:31
  117.5 3.1 %collective-permute-start.21 = (f32[2,8,256]{2,1,0:T(8,128)S(1)}, f32[2,8,256]{2,1,0:T(8,128)S(1)}, u32[]{:S(2)}, u32[]{:S(2)}) collective-permute-start(f32[2,8,256]{2,1,0:T(8,128)S(1)} %get-tuple-element.281), channel_id=1, source_target_pairs={{0,22},{2,20},{4,18},{6,16},{8,30},{10,28},{12,26},{14,24},{16,6},... | collective-permute-start | bytes 49160 | tf_op jit(solution)/shard_map/ppermute | solution.py:31
  121.7 2.6 %collective-permute-start.23 = (f32[2,8,256]{2,1,0:T(8,128)S(1)}, f32[2,8,256]{2,1,0:T(8,128)S(1)}, u32[]{:S(2)}, u32[]{:S(2)}) collective-permute-start(f32[2,8,256]{2,1,0:T(8,128)S(1)} %get-tuple-element.294), channel_id=1, source_target_pairs={{0,26},{2,24},{4,30},{6,28},{8,18},{10,16},{12,22},{14,20},{16,10}... | collective-permute-start | bytes 49160 | tf_op jit(solution)/shard_map/ppermute | solution.py:31
  126.0 3.0 %collective-permute-start.25 = (f32[2,8,256]{2,1,0:T(8,128)S(1)}, f32[2,8,256]{2,1,0:T(8,128)S(1)}, u32[]{:S(2)}, u32[]{:S(2)}) collective-permute-start(f32[2,8,256]{2,1,0:T(8,128)S(1)} %get-tuple-element.279), channel_id=1, source_target_pairs={{0,30},{2,28},{4,26},{6,24},{8,22},{10,20},{12,18},{14,16},{16,14}... | collective-permute-start | bytes 49160 | tf_op jit(solution)/shard_map/ppermute | solution.py:31
  129.2 1.7 %collective-permute-done.24 = f32[2,8,256]{2,1,0:T(8,128)S(1)} collective-permute-done((f32[2,8,256]{2,1,0:T(8,128)S(1)}, f32[2,8,256]{2,1,0:T(8,128)S(1)}, u32[]{:S(2)}, u32[]{:S(2)}) %collective-permute-start.24) | collective-permute-done | bytes 16416 | tf_op jit(solution)/shard_map/ppermute | solution.py:31
  132.5 14.4 %all_to_all.45 = f32[32,8,256]{2,1,0:T(8,128)S(1)} all-to-all(f32[32,8,256]{2,1,0:T(8,128)S(1)} %copy.108), channel_id=1, replica_groups=mesh['tm'=16,'band'=2] {'tm'}, dimensions={0} | all-to-all | bytes 524288 | tf_op jit(solution)/shard_map/all_to_all | solution.py:174
  148.1 1.7 %collective-permute-start.26 = (f32[2,1,256]{2,1,0:T(1,128)S(1)}, f32[2,1,256]{2,1,0:T(1,128)S(1)}, u32[]{:S(2)}, u32[]{:S(2)}) collective-permute-start(f32[2,1,256]{2,1,0:T(1,128)S(1)} %get-tuple-element.265), channel_id=1, source_target_pairs={{0,1},{1,0},{2,3},{3,2},{4,5},{5,4},{6,7},{7,6},{8,9},{9,8},{10,11... | collective-permute-start | bytes 6152 | tf_op jit(solution)/shard_map/ppermute | solution.py:43
  153.6 7.2 %collective-permute-done.28 = f32[1,128,256]{2,1,0:T(8,128)S(1)} collective-permute-done((f32[1,128,256]{2,1,0:T(8,128)S(1)}, f32[1,128,256]{2,1,0:T(8,128)S(1)}, u32[]{:S(2)}, u32[]{:S(2)}) %collective-permute-start.28) | collective-permute-done | bytes 131104 | tf_op jit(solution)/shard_map/ppermute | solution.py:51
  160.9 2.5 %collective-permute-done.29 = f32[1,128,256]{2,1,0:T(8,128)S(1)} collective-permute-done((f32[1,128,256]{2,1,0:T(8,128)S(1)}, f32[1,128,256]{2,1,0:T(8,128)S(1)}, u32[]{:S(2)}, u32[]{:S(2)}) %collective-permute-start.29) | collective-permute-done | bytes 131104 | tf_op jit(solution)/shard_map/ppermute | solution.py:51
  (289 shorter events, 60.5 us)
Async XLA Ops:
  1.7 9.6 %collective-permute-start.3 = (f32[1,128,256]{2,1,0:T(8,128)S(1)}, f32[1,128,256]{2,1,0:T(8,128)S(1)}, u32[]{:S(2)}, u32[]{:S(2)}) collective-permute-start(f32[1,128,256]{2,1,0:T(8,128)S(1)} %get-tuple-element.329), channel_id=1, source_target_pairs={{0,2},{2,4},{4,6},{6,8},{8,10},{10,12},{12,14},{14,16},{16,18},{18... | collective-permute-start | bytes 393224 | tf_op jit(solution)/shard_map/ppermute | solution.py:43
  2.2 9.0 %collective-permute-start.4 = (f32[1,128,256]{2,1,0:T(8,128)S(1)}, f32[1,128,256]{2,1,0:T(8,128)S(1)}, u32[]{:S(2)}, u32[]{:S(2)}) collective-permute-start(f32[1,128,256]{2,1,0:T(8,128)S(1)} %get-tuple-element.330), channel_id=1, source_target_pairs={{2,0},{4,2},{6,4},{8,6},{10,8},{12,10},{14,12},{16,14},{18,16},{20... | collective-permute-start | bytes 393224 | tf_op jit(solution)/shard_map/ppermute | solution.py:44
  18.6 7.2 %collective-permute-start.7 = (f32[1,128,256]{2,1,0:T(8,128)S(1)}, f32[1,128,256]{2,1,0:T(8,128)S(1)}, u32[]{:S(2)}, u32[]{:S(2)}) collective-permute-start(f32[1,128,256]{2,1,0:T(8,128)S(1)} %get-tuple-element.311), channel_id=1, source_target_pairs={{0,2},{2,4},{4,6},{6,8},{8,10},{10,12},{12,14},{14,16},{16,18},{18... | collective-permute-start | bytes 393224 | tf_op jit(solution)/shard_map/ppermute | solution.py:51
  35.3 14.7 %all-to-all-start = ((f32[2,128,256]{2,0,1:T(2,128)}), f32[2,128,256]{2,0,1:T(2,128)S(1)}, u32[]{:S(2)}, u32[]{:S(2)}) async-start(f32[2,128,256]{2,0,1:T(2,128)} %copy.87), calls=%async_computation | async-start | bytes 524288 | tf_op jit(solution)/shard_map/all_to_all | solution.py:144
  51.6 13.5 %all-to-all-start.1 = ((f32[32,8,256]{2,1,0:T(8,128)}), f32[32,8,256]{2,1,0:T(8,128)S(1)}, u32[]{:S(2)}, u32[]{:S(2)}) async-start(f32[32,8,256]{2,1,0:T(8,128)} %copy.90), calls=%async_computation.1 | async-start | bytes 524288 | tf_op jit(solution)/shard_map/all_to_all | solution.py:145
  65.3 3.8 %collective-permute-start = (f32[2,2,4,256]{3,2,1,0:T(4,128)S(1)}, f32[2,2,4,256]{3,2,1,0:T(4,128)S(1)}, u32[]{:S(2)}, u32[]{:S(2)}) collective-permute-start(f32[2,2,4,256]{3,2,1,0:T(4,128)S(1)} %get-tuple-element.420), channel_id=1, source_target_pairs={{1,0},{0,1},{3,2},{2,3},{5,4},{4,5},{7,6},{6,7},{9,8},{8,9},{11,10... | collective-permute-start | bytes 49160 | tf_op jit(solution)/shard_map/while/body/eval_jaxpr/ppermute | solution.py:44
  67.0 3.7 %collective-permute-start.1 = (f32[2,2,4,256]{3,2,1,0:T(4,128)S(1)}, f32[2,2,4,256]{3,2,1,0:T(4,128)S(1)}, u32[]{:S(2)}, u32[]{:S(2)}) collective-permute-start(f32[2,2,4,256]{3,2,1,0:T(4,128)S(1)} %get-tuple-element.421), channel_id=1, source_target_pairs={{0,1},{1,0},{2,3},{3,2},{4,5},{5,4},{6,7},{7,6},{8,9},{9,8},{10,11... | collective-permute-start | bytes 49160 | tf_op jit(solution)/shard_map/while/body/eval_jaxpr/ppermute | solution.py:43
  73.0 3.8 %collective-permute-start = (f32[2,2,4,256]{3,2,1,0:T(4,128)S(1)}, f32[2,2,4,256]{3,2,1,0:T(4,128)S(1)}, u32[]{:S(2)}, u32[]{:S(2)}) collective-permute-start(f32[2,2,4,256]{3,2,1,0:T(4,128)S(1)} %get-tuple-element.420), channel_id=1, source_target_pairs={{1,0},{0,1},{3,2},{2,3},{5,4},{4,5},{7,6},{6,7},{9,8},{8,9},{11,10... | collective-permute-start | bytes 49160 | tf_op jit(solution)/shard_map/while/body/eval_jaxpr/ppermute | solution.py:44
  73.4 3.7 %collective-permute-start.1 = (f32[2,2,4,256]{3,2,1,0:T(4,128)S(1)}, f32[2,2,4,256]{3,2,1,0:T(4,128)S(1)}, u32[]{:S(2)}, u32[]{:S(2)}) collective-permute-start(f32[2,2,4,256]{3,2,1,0:T(4,128)S(1)} %get-tuple-element.421), channel_id=1, source_target_pairs={{0,1},{1,0},{2,3},{3,2},{4,5},{5,4},{6,7},{7,6},{8,9},{9,8},{10,11... | collective-permute-start | bytes 49160 | tf_op jit(solution)/shard_map/while/body/eval_jaxpr/ppermute | solution.py:43
  79.3 3.8 %collective-permute-start = (f32[2,2,4,256]{3,2,1,0:T(4,128)S(1)}, f32[2,2,4,256]{3,2,1,0:T(4,128)S(1)}, u32[]{:S(2)}, u32[]{:S(2)}) collective-permute-start(f32[2,2,4,256]{3,2,1,0:T(4,128)S(1)} %get-tuple-element.420), channel_id=1, source_target_pairs={{1,0},{0,1},{3,2},{2,3},{5,4},{4,5},{7,6},{6,7},{9,8},{8,9},{11,10... | collective-permute-start | bytes 49160 | tf_op jit(solution)/shard_map/while/body/eval_jaxpr/ppermute | solution.py:44
  81.1 3.7 %collective-permute-start.1 = (f32[2,2,4,256]{3,2,1,0:T(4,128)S(1)}, f32[2,2,4,256]{3,2,1,0:T(4,128)S(1)}, u32[]{:S(2)}, u32[]{:S(2)}) collective-permute-start(f32[2,2,4,256]{3,2,1,0:T(4,128)S(1)} %get-tuple-element.421), channel_id=1, source_target_pairs={{0,1},{1,0},{2,3},{3,2},{4,5},{5,4},{6,7},{7,6},{8,9},{9,8},{10,11... | collective-permute-start | bytes 49160 | tf_op jit(solution)/shard_map/while/body/eval_jaxpr/ppermute | solution.py:43
  87.0 3.8 %collective-permute-start = (f32[2,2,4,256]{3,2,1,0:T(4,128)S(1)}, f32[2,2,4,256]{3,2,1,0:T(4,128)S(1)}, u32[]{:S(2)}, u32[]{:S(2)}) collective-permute-start(f32[2,2,4,256]{3,2,1,0:T(4,128)S(1)} %get-tuple-element.420), channel_id=1, source_target_pairs={{1,0},{0,1},{3,2},{2,3},{5,4},{4,5},{7,6},{6,7},{9,8},{8,9},{11,10... | collective-permute-start | bytes 49160 | tf_op jit(solution)/shard_map/while/body/eval_jaxpr/ppermute | solution.py:44
  87.4 3.7 %collective-permute-start.1 = (f32[2,2,4,256]{3,2,1,0:T(4,128)S(1)}, f32[2,2,4,256]{3,2,1,0:T(4,128)S(1)}, u32[]{:S(2)}, u32[]{:S(2)}) collective-permute-start(f32[2,2,4,256]{3,2,1,0:T(4,128)S(1)} %get-tuple-element.421), channel_id=1, source_target_pairs={{0,1},{1,0},{2,3},{3,2},{4,5},{5,4},{6,7},{7,6},{8,9},{9,8},{10,11... | collective-permute-start | bytes 49160 | tf_op jit(solution)/shard_map/while/body/eval_jaxpr/ppermute | solution.py:43
  93.4 3.8 %collective-permute-start = (f32[2,2,4,256]{3,2,1,0:T(4,128)S(1)}, f32[2,2,4,256]{3,2,1,0:T(4,128)S(1)}, u32[]{:S(2)}, u32[]{:S(2)}) collective-permute-start(f32[2,2,4,256]{3,2,1,0:T(4,128)S(1)} %get-tuple-element.420), channel_id=1, source_target_pairs={{1,0},{0,1},{3,2},{2,3},{5,4},{4,5},{7,6},{6,7},{9,8},{8,9},{11,10... | collective-permute-start | bytes 49160 | tf_op jit(solution)/shard_map/while/body/eval_jaxpr/ppermute | solution.py:44
  95.1 3.7 %collective-permute-start.1 = (f32[2,2,4,256]{3,2,1,0:T(4,128)S(1)}, f32[2,2,4,256]{3,2,1,0:T(4,128)S(1)}, u32[]{:S(2)}, u32[]{:S(2)}) collective-permute-start(f32[2,2,4,256]{3,2,1,0:T(4,128)S(1)} %get-tuple-element.421), channel_id=1, source_target_pairs={{0,1},{1,0},{2,3},{3,2},{4,5},{5,4},{6,7},{7,6},{8,9},{9,8},{10,11... | collective-permute-start | bytes 49160 | tf_op jit(solution)/shard_map/while/body/eval_jaxpr/ppermute | solution.py:43
  101.1 3.8 %collective-permute-start = (f32[2,2,4,256]{3,2,1,0:T(4,128)S(1)}, f32[2,2,4,256]{3,2,1,0:T(4,128)S(1)}, u32[]{:S(2)}, u32[]{:S(2)}) collective-permute-start(f32[2,2,4,256]{3,2,1,0:T(4,128)S(1)} %get-tuple-element.420), channel_id=1, source_target_pairs={{1,0},{0,1},{3,2},{2,3},{5,4},{4,5},{7,6},{6,7},{9,8},{8,9},{11,10... | collective-permute-start | bytes 49160 | tf_op jit(solution)/shard_map/while/body/eval_jaxpr/ppermute | solution.py:44
  101.5 3.7 %collective-permute-start.1 = (f32[2,2,4,256]{3,2,1,0:T(4,128)S(1)}, f32[2,2,4,256]{3,2,1,0:T(4,128)S(1)}, u32[]{:S(2)}, u32[]{:S(2)}) collective-permute-start(f32[2,2,4,256]{3,2,1,0:T(4,128)S(1)} %get-tuple-element.421), channel_id=1, source_target_pairs={{0,1},{1,0},{2,3},{3,2},{4,5},{5,4},{6,7},{7,6},{8,9},{9,8},{10,11... | collective-permute-start | bytes 49160 | tf_op jit(solution)/shard_map/while/body/eval_jaxpr/ppermute | solution.py:43
  107.6 4.2 %collective-permute-start.12 = (f32[2,8,256]{2,1,0:T(8,128)S(1)}, f32[2,8,256]{2,1,0:T(8,128)S(1)}, u32[]{:S(2)}, u32[]{:S(2)}) collective-permute-start(f32[2,8,256]{2,1,0:T(8,128)S(1)} %get-tuple-element.290), channel_id=1, source_target_pairs={{0,4},{2,6},{4,0},{6,2},{8,12},{10,14},{12,8},{14,10},{16,20},{18,... | collective-permute-start | bytes 49160 | tf_op jit(solution)/shard_map/ppermute | solution.py:31
  107.7 6.4 %collective-permute-start.13 = (f32[2,8,256]{2,1,0:T(8,128)S(1)}, f32[2,8,256]{2,1,0:T(8,128)S(1)}, u32[]{:S(2)}, u32[]{:S(2)}) collective-permute-start(f32[2,8,256]{2,1,0:T(8,128)S(1)} %get-tuple-element.289), channel_id=1, source_target_pairs={{0,6},{2,4},{4,2},{6,0},{8,14},{10,12},{12,10},{14,8},{16,22},{18,... | collective-permute-start | bytes 49160 | tf_op jit(solution)/shard_map/ppermute | solution.py:31
  109.5 5.7 %collective-permute-start.14 = (f32[2,8,256]{2,1,0:T(8,128)S(1)}, f32[2,8,256]{2,1,0:T(8,128)S(1)}, u32[]{:S(2)}, u32[]{:S(2)}) collective-permute-start(f32[2,8,256]{2,1,0:T(8,128)S(1)} %get-tuple-element.288), channel_id=1, source_target_pairs={{0,8},{2,10},{4,12},{6,14},{8,0},{10,2},{12,4},{14,6},{16,24},{18,... | collective-permute-start | bytes 49160 | tf_op jit(solution)/shard_map/ppermute | solution.py:31
  109.5 7.4 %collective-permute-start.15 = (f32[2,8,256]{2,1,0:T(8,128)S(1)}, f32[2,8,256]{2,1,0:T(8,128)S(1)}, u32[]{:S(2)}, u32[]{:S(2)}) collective-permute-start(f32[2,8,256]{2,1,0:T(8,128)S(1)} %get-tuple-element.287), channel_id=1, source_target_pairs={{0,10},{2,8},{4,14},{6,12},{8,2},{10,0},{12,6},{14,4},{16,26},{18,... | collective-permute-start | bytes 49160 | tf_op jit(solution)/shard_map/ppermute | solution.py:31
  111.2 6.3 %collective-permute-start.16 = (f32[2,8,256]{2,1,0:T(8,128)S(1)}, f32[2,8,256]{2,1,0:T(8,128)S(1)}, u32[]{:S(2)}, u32[]{:S(2)}) collective-permute-start(f32[2,8,256]{2,1,0:T(8,128)S(1)} %get-tuple-element.286), channel_id=1, source_target_pairs={{0,12},{2,14},{4,8},{6,10},{8,4},{10,6},{12,0},{14,2},{16,28},{18,... | collective-permute-start | bytes 49160 | tf_op jit(solution)/shard_map/ppermute | solution.py:31
  111.8 8.8 %collective-permute-start.17 = (f32[2,8,256]{2,1,0:T(8,128)S(1)}, f32[2,8,256]{2,1,0:T(8,128)S(1)}, u32[]{:S(2)}, u32[]{:S(2)}) collective-permute-start(f32[2,8,256]{2,1,0:T(8,128)S(1)} %get-tuple-element.285), channel_id=1, source_target_pairs={{0,14},{2,12},{4,10},{6,8},{8,6},{10,4},{12,2},{14,0},{16,30},{18,... | collective-permute-start | bytes 49160 | tf_op jit(solution)/shard_map/ppermute | solution.py:31
  114.1 7.6 %collective-permute-start.18 = (f32[2,8,256]{2,1,0:T(8,128)S(1)}, f32[2,8,256]{2,1,0:T(8,128)S(1)}, u32[]{:S(2)}, u32[]{:S(2)}) collective-permute-start(f32[2,8,256]{2,1,0:T(8,128)S(1)} %get-tuple-element.284), channel_id=1, source_target_pairs={{0,16},{2,18},{4,20},{6,22},{8,24},{10,26},{12,28},{14,30},{16,0},... | collective-permute-start | bytes 49160 | tf_op jit(solution)/shard_map/ppermute | solution.py:31
  115.2 9.2 %collective-permute-start.19 = (f32[2,8,256]{2,1,0:T(8,128)S(1)}, f32[2,8,256]{2,1,0:T(8,128)S(1)}, u32[]{:S(2)}, u32[]{:S(2)}) collective-permute-start(f32[2,8,256]{2,1,0:T(8,128)S(1)} %get-tuple-element.283), channel_id=1, source_target_pairs={{0,18},{2,16},{4,22},{6,20},{8,26},{10,24},{12,30},{14,28},{16,2},... | collective-permute-start | bytes 49160 | tf_op jit(solution)/shard_map/ppermute | solution.py:31
  116.9 9.1 %collective-permute-start.20 = (f32[2,8,256]{2,1,0:T(8,128)S(1)}, f32[2,8,256]{2,1,0:T(8,128)S(1)}, u32[]{:S(2)}, u32[]{:S(2)}) collective-permute-start(f32[2,8,256]{2,1,0:T(8,128)S(1)} %get-tuple-element.282), channel_id=1, source_target_pairs={{0,20},{2,22},{4,16},{6,18},{8,28},{10,30},{12,24},{14,26},{16,4},... | collective-permute-start | bytes 49160 | tf_op jit(solution)/shard_map/ppermute | solution.py:31
  117.5 11.5 %collective-permute-start.21 = (f32[2,8,256]{2,1,0:T(8,128)S(1)}, f32[2,8,256]{2,1,0:T(8,128)S(1)}, u32[]{:S(2)}, u32[]{:S(2)}) collective-permute-start(f32[2,8,256]{2,1,0:T(8,128)S(1)} %get-tuple-element.281), channel_id=1, source_target_pairs={{0,22},{2,20},{4,18},{6,16},{8,30},{10,28},{12,26},{14,24},{16,6},... | collective-permute-start | bytes 49160 | tf_op jit(solution)/shard_map/ppermute | solution.py:31
  120.7 8.4 %collective-permute-start.22 = (f32[2,8,256]{2,1,0:T(8,128)S(1)}, f32[2,8,256]{2,1,0:T(8,128)S(1)}, u32[]{:S(2)}, u32[]{:S(2)}) collective-permute-start(f32[2,8,256]{2,1,0:T(8,128)S(1)} %get-tuple-element.280), channel_id=1, source_target_pairs={{0,24},{2,26},{4,28},{6,30},{8,16},{10,18},{12,20},{14,22},{16,8},... | collective-permute-start | bytes 49160 | tf_op jit(solution)/shard_map/ppermute | solution.py:31
  121.7 7.4 %collective-permute-start.23 = (f32[2,8,256]{2,1,0:T(8,128)S(1)}, f32[2,8,256]{2,1,0:T(8,128)S(1)}, u32[]{:S(2)}, u32[]{:S(2)}) collective-permute-start(f32[2,8,256]{2,1,0:T(8,128)S(1)} %get-tuple-element.294), channel_id=1, source_target_pairs={{0,26},{2,24},{4,30},{6,28},{8,18},{10,16},{12,22},{14,20},{16,10}... | collective-permute-start | bytes 49160 | tf_op jit(solution)/shard_map/ppermute | solution.py:31
  124.4 6.5 %collective-permute-start.24 = (f32[2,8,256]{2,1,0:T(8,128)S(1)}, f32[2,8,256]{2,1,0:T(8,128)S(1)}, u32[]{:S(2)}, u32[]{:S(2)}) collective-permute-start(f32[2,8,256]{2,1,0:T(8,128)S(1)} %get-tuple-element.293), channel_id=1, source_target_pairs={{0,28},{2,30},{4,24},{6,26},{8,20},{10,22},{12,16},{14,18},{16,12}... | collective-permute-start | bytes 49160 | tf_op jit(solution)/shard_map/ppermute | solution.py:31
  126.0 5.9 %collective-permute-start.25 = (f32[2,8,256]{2,1,0:T(8,128)S(1)}, f32[2,8,256]{2,1,0:T(8,128)S(1)}, u32[]{:S(2)}, u32[]{:S(2)}) collective-permute-start(f32[2,8,256]{2,1,0:T(8,128)S(1)} %get-tuple-element.279), channel_id=1, source_target_pairs={{0,30},{2,28},{4,26},{6,24},{8,22},{10,20},{12,18},{14,16},{16,14}... | collective-permute-start | bytes 49160 | tf_op jit(solution)/shard_map/ppermute | solution.py:31
  153.5 7.2 %collective-permute-start.28 = (f32[1,128,256]{2,1,0:T(8,128)S(1)}, f32[1,128,256]{2,1,0:T(8,128)S(1)}, u32[]{:S(2)}, u32[]{:S(2)}) collective-permute-start(f32[1,128,256]{2,1,0:T(8,128)S(1)} %get-tuple-element.263), channel_id=1, source_target_pairs={{0,2},{2,4},{4,6},{6,8},{8,10},{10,12},{12,14},{14,16},{16,18},{18... | collective-permute-start | bytes 393224 | tf_op jit(solution)/shard_map/ppermute | solution.py:51
  (18 other events, 73.2 us)
